TPU v7x, 32 devices: a whole 2x2x4 slice. The times are simulated.
32 devices in a mesh: dp: 8 (over z, x), fsdp: 4 (over y, core).
Axes of the slice: x: 2, y: 2, z: 4, core: 2. Of those that a mesh axis runs over, the one named last changes fastest.
Arguments:
- latents: float32 [96, 256, 384], P(('dp', 'fsdp')), may hold values from -6 to 6
- conditioning: float32 [96, 384], P(('dp', 'fsdp')), may hold values from -6 to 6
- seq_counts: int32 [32], P(('dp', 'fsdp')), may hold values from 1 to 3, as said below
- cotangent: float32 [96, 256, 384], P(('dp', 'fsdp')), may hold values from -6 to 6
- ada_weight: bfloat16 [2, 384, 2304], P(None, 'fsdp'), may hold values from -0.3125 to 0.3125
- ada_bias: bfloat16 [2, 2304], P(None, 'fsdp'), may hold values from -2.390625 to 2.390625
- qkv_weight: bfloat16 [2, 384, 1152], P(None, 'fsdp'), may hold values from -0.3125 to 0.3125
- proj_weight: bfloat16 [2, 384, 384], P(None, 'fsdp'), may hold values from -6 to 6
- proj_bias: bfloat16 [2, 384], P(None, 'fsdp'), may hold values from -3.59375 to 3.59375
- up_weight: bfloat16 [2, 384, 1536], P(None, 'fsdp'), may hold values from -0.3125 to 0.3125
- up_bias: bfloat16 [2, 1536], P(None, 'fsdp'), may hold values from -3.59375 to 3.59375
- down_weight: bfloat16 [2, 1536, 384], P(None, 'fsdp'), may hold values from -0.15625 to 0.15625
- down_bias: bfloat16 [2, 384], P(None, 'fsdp'), may hold values from -3.59375 to 3.59375
Outputs:
- block_out: float32 [96, 256, 384], P(('dp', 'fsdp'))
- grad_latents: float32 [96, 256, 384], P(('dp', 'fsdp'))
- grad_conditioning: float32 [96, 384], P(('dp', 'fsdp'))
- grad_ada_weight: float32 [2, 384, 2304], P(None, 'fsdp')
- grad_ada_bias: float32 [2, 2304], P(None, 'fsdp')
- grad_qkv_weight: float32 [2, 384, 1152], P(None, 'fsdp')
- grad_proj_weight: float32 [2, 384, 384], P(None, 'fsdp')
- grad_proj_bias: float32 [2, 384], P(None, 'fsdp')
- grad_up_weight: float32 [2, 384, 1536], P(None, 'fsdp')
- grad_up_bias: float32 [2, 1536], P(None, 'fsdp')
- grad_down_weight: float32 [2, 1536, 384], P(None, 'fsdp')
- grad_down_bias: float32 [2, 384], P(None, 'fsdp')
Inputs may be any that keep to these rules, and one draw needn't show every extreme that they name: `seq_counts`: number of live sequences of a device; its slots from that number on are padding.
All inputs are finite; a program needn't handle non-finite values.
Results may differ from a plain program's by a relative error of at most 0.014.
Values may be sent and summed in bfloat16 or wider, within the bound.
No kernel may reach another device: no remote copies, remote signals or barrier semaphores. Data moves between devices by JAX's collectives and lax.ppermute only.
A program may use at most 192 MiB of HBM per device.

v0:
```python
import jax
import jax.numpy as jnp
from jax import lax
from jax.sharding import PartitionSpec as P

HEADS = 6
LAYERS = 2
NORM_EPS = 1e-06
GELU_K = 0.7978845608028654
GELU_C = 0.044715


def einsum_mixed(form, left, right):
    return jnp.einsum(form, left, right, preferred_element_type=jnp.float32)


def matmul_last(left, right):
    flat = left.reshape(-1, left.shape[-1])
    return jnp.dot(flat, right, preferred_element_type=jnp.float32).reshape(
        left.shape[:-1] + (right.shape[1],)
    )


def matmul_back(left, right):
    flat = left.reshape(-1, left.shape[-1])
    return jnp.dot(flat, right.T, preferred_element_type=jnp.float32).reshape(
        left.shape[:-1] + (right.shape[0],)
    )


def outer_total(left, right):
    return jnp.dot(
        left.reshape(-1, left.shape[-1]).T,
        right.reshape(-1, right.shape[-1]),
        preferred_element_type=jnp.float32,
    )


def norm_rows(values):
    center = values - jnp.mean(values, axis=-1, keepdims=True)
    inv_std = lax.rsqrt(jnp.mean(center * center, axis=-1, keepdims=True) + NORM_EPS)
    return (center * inv_std, inv_std)


def norm_back(normed, inv_std, grad_normed):
    mean_grad = jnp.mean(grad_normed, axis=-1, keepdims=True)
    mean_prod = jnp.mean(grad_normed * normed, axis=-1, keepdims=True)
    return inv_std * (grad_normed - mean_grad - normed * mean_prod)


def gelu_tanh(values):
    inner = GELU_K * (values + GELU_C * values * values * values)
    return 0.5 * values * (1.0 + jnp.tanh(inner))


def gelu_slope(values):
    tangent = jnp.tanh(GELU_K * (values + GELU_C * values * values * values))
    return 0.5 * (1.0 + tangent) + 0.5 * values * (1.0 - tangent * tangent) * GELU_K * (
        1.0 + 3.0 * GELU_C * values * values
    )


def silu_slope(values):
    sigm = jax.nn.sigmoid(values)
    return sigm * (1.0 + values * (1.0 - sigm))


def split_heads(qkv):
    seq_slots, length, triple = qkv.shape
    width = triple // 3
    split = qkv.reshape(seq_slots, length, 3, HEADS, width // HEADS)
    return (split[:, :, 0], split[:, :, 1], split[:, :, 2])


def attend(qkv):
    queries, keys, values = split_heads(qkv)
    scale = 1.0 / jnp.sqrt(jnp.float32(queries.shape[-1]))
    scores = einsum_mixed("sqhd,skhd->shqk", queries, keys) * scale
    top = jnp.max(scores, axis=-1, keepdims=True)
    expo = jnp.exp(scores - top)
    probs = expo / jnp.sum(expo, axis=-1, keepdims=True)
    probs_low = probs.astype(jnp.bfloat16)
    mixed = einsum_mixed("shqk,skhd->sqhd", probs_low, values).astype(jnp.bfloat16)
    return (probs, probs_low, mixed.reshape(qkv.shape[0], qkv.shape[1], -1))


def attend_back(qkv, probs, probs_low, grad_mixed):
    queries, keys, values = split_heads(qkv)
    scale = 1.0 / jnp.sqrt(jnp.float32(queries.shape[-1]))
    grad_heads = grad_mixed.reshape(values.shape)
    grad_probs = einsum_mixed("sqhd,skhd->shqk", grad_heads, values)
    grad_values = einsum_mixed("shqk,sqhd->skhd", probs_low, grad_heads)
    row_dot = jnp.sum(probs * grad_probs, axis=-1, keepdims=True)
    grad_scores = (probs * (grad_probs - row_dot) * scale).astype(jnp.bfloat16)
    grad_queries = einsum_mixed("shqk,skhd->sqhd", grad_scores, keys)
    grad_keys = einsum_mixed("shqk,sqhd->skhd", grad_scores, queries)
    joined = jnp.stack([grad_queries, grad_keys, grad_values], axis=2)
    return joined.reshape(qkv.shape).astype(jnp.bfloat16)


def layer_parts(resid, cond, weights):
    (
        ada_weight,
        ada_bias,
        qkv_weight,
        proj_weight,
        proj_bias,
        up_weight,
        up_bias,
        down_weight,
        down_bias,
    ) = weights
    width = resid.shape[-1]
    act_low = jax.nn.silu(cond).astype(jnp.bfloat16)
    ada = jnp.dot(act_low, ada_weight, preferred_element_type=jnp.float32) + ada_bias.astype(
        jnp.float32
    )
    mods = [ada[:, None, piece_idx * width : (piece_idx + 1) * width] for piece_idx in range(6)]
    normed_one, inv_one = norm_rows(resid)
    attn_in = (normed_one * (1.0 + mods[1]) + mods[0]).astype(jnp.bfloat16)
    qkv = matmul_last(attn_in, qkv_weight).astype(jnp.bfloat16)
    probs, probs_low, mixed = attend(qkv)
    attn = matmul_last(mixed, proj_weight) + proj_bias.astype(jnp.float32)
    resid_one = resid + mods[2] * attn
    normed_two, inv_two = norm_rows(resid_one)
    mlp_in = (normed_two * (1.0 + mods[4]) + mods[3]).astype(jnp.bfloat16)
    pre_act = matmul_last(mlp_in, up_weight) + up_bias.astype(jnp.float32)
    hidden = gelu_tanh(pre_act).astype(jnp.bfloat16)
    branch = matmul_last(hidden, down_weight) + down_bias.astype(jnp.float32)
    result = resid_one + mods[5] * branch
    return dict(
        act_low=act_low,
        mods=mods,
        normed_one=normed_one,
        inv_one=inv_one,
        attn_in=attn_in,
        qkv=qkv,
        probs=probs,
        probs_low=probs_low,
        mixed=mixed,
        attn=attn,
        normed_two=normed_two,
        inv_two=inv_two,
        mlp_in=mlp_in,
        pre_act=pre_act,
        hidden=hidden,
        branch=branch,
        result=result,
    )


def layer_backward(resid, cond, weights, grad_out):
    (
        ada_weight,
        ada_bias,
        qkv_weight,
        proj_weight,
        proj_bias,
        up_weight,
        up_bias,
        down_weight,
        down_bias,
    ) = weights
    saved = layer_parts(resid, cond, weights)
    mods = saved["mods"]
    grad_gate_two = jnp.sum(grad_out * saved["branch"], axis=1)
    grad_branch = grad_out * mods[5]
    grad_down_bias = jnp.sum(grad_branch, axis=(0, 1))
    branch_low = grad_branch.astype(jnp.bfloat16)
    grad_down_weight = outer_total(saved["hidden"], branch_low)
    grad_pre = matmul_back(branch_low, down_weight) * gelu_slope(saved["pre_act"])
    grad_up_bias = jnp.sum(grad_pre, axis=(0, 1))
    pre_low = grad_pre.astype(jnp.bfloat16)
    grad_up_weight = outer_total(saved["mlp_in"], pre_low)
    grad_mlp = matmul_back(pre_low, up_weight)
    grad_shift_two = jnp.sum(grad_mlp, axis=1)
    grad_scale_two = jnp.sum(grad_mlp * saved["normed_two"], axis=1)
    grad_one = grad_out + norm_back(
        saved["normed_two"], saved["inv_two"], grad_mlp * (1.0 + mods[4])
    )
    grad_gate_one = jnp.sum(grad_one * saved["attn"], axis=1)
    grad_attn = grad_one * mods[2]
    grad_proj_bias = jnp.sum(grad_attn, axis=(0, 1))
    attn_low = grad_attn.astype(jnp.bfloat16)
    grad_proj_weight = outer_total(saved["mixed"], attn_low)
    grad_mixed = matmul_back(attn_low, proj_weight).astype(jnp.bfloat16)
    grad_qkv = attend_back(saved["qkv"], saved["probs"], saved["probs_low"], grad_mixed)
    grad_qkv_weight = outer_total(saved["attn_in"], grad_qkv)
    grad_in = matmul_back(grad_qkv, qkv_weight)
    grad_shift_one = jnp.sum(grad_in, axis=1)
    grad_scale_one = jnp.sum(grad_in * saved["normed_one"], axis=1)
    grad_resid = grad_one + norm_back(
        saved["normed_one"], saved["inv_one"], grad_in * (1.0 + mods[1])
    )
    grad_ada = jnp.concatenate(
        [
            grad_shift_one,
            grad_scale_one,
            grad_gate_one,
            grad_shift_two,
            grad_scale_two,
            grad_gate_two,
        ],
        axis=-1,
    )
    grad_ada_bias = jnp.sum(grad_ada, axis=0)
    ada_low = grad_ada.astype(jnp.bfloat16)
    grad_ada_weight = jnp.dot(saved["act_low"].T, ada_low, preferred_element_type=jnp.float32)
    grad_cond = jnp.dot(ada_low, ada_weight.T, preferred_element_type=jnp.float32) * silu_slope(
        cond
    )
    grads = (
        grad_ada_weight,
        grad_ada_bias,
        grad_qkv_weight,
        grad_proj_weight,
        grad_proj_bias,
        grad_up_weight,
        grad_up_bias,
        grad_down_weight,
        grad_down_bias,
    )
    return (grad_resid, grad_cond, grads)


def gather_forward(stacks, layer_idx):
    (
        ada_weight,
        ada_bias,
        qkv_weight,
        proj_weight,
        proj_bias,
        up_weight,
        up_bias,
        down_weight,
        down_bias,
    ) = stacks
    return (
        lax.all_gather(ada_weight[layer_idx], "fsdp", axis=0, tiled=True),
        lax.all_gather(ada_bias[layer_idx], "fsdp", axis=0, tiled=True),
        lax.all_gather(qkv_weight[layer_idx], "fsdp", axis=0, tiled=True),
        lax.all_gather(proj_weight[layer_idx], "fsdp", axis=0, tiled=True),
        lax.all_gather(proj_bias[layer_idx], "fsdp", axis=0, tiled=True),
        lax.all_gather(up_weight[layer_idx], "fsdp", axis=0, tiled=True),
        lax.all_gather(up_bias[layer_idx], "fsdp", axis=0, tiled=True),
        lax.all_gather(down_weight[layer_idx], "fsdp", axis=0, tiled=True),
        lax.all_gather(down_bias[layer_idx], "fsdp", axis=0, tiled=True),
    )


def gather_backward(stacks, layer_idx):
    (
        ada_weight,
        ada_bias,
        qkv_weight,
        proj_weight,
        proj_bias,
        up_weight,
        up_bias,
        down_weight,
        down_bias,
    ) = stacks
    return (
        lax.all_gather(ada_weight[layer_idx], "fsdp", axis=0, tiled=True),
        lax.all_gather(ada_bias[layer_idx], "fsdp", axis=0, tiled=True),
        lax.all_gather(qkv_weight[layer_idx], "fsdp", axis=0, tiled=True),
        lax.all_gather(proj_weight[layer_idx], "fsdp", axis=0, tiled=True),
        lax.all_gather(proj_bias[layer_idx], "fsdp", axis=0, tiled=True),
        lax.all_gather(up_weight[layer_idx], "fsdp", axis=0, tiled=True),
        lax.all_gather(up_bias[layer_idx], "fsdp", axis=0, tiled=True),
        lax.all_gather(down_weight[layer_idx], "fsdp", axis=0, tiled=True),
        lax.all_gather(down_bias[layer_idx], "fsdp", axis=0, tiled=True),
    )


def reduce_layer(grads):
    shards = (
        lax.psum_scatter(grads[0], "fsdp", scatter_dimension=0, tiled=True),
        lax.psum_scatter(grads[1], "fsdp", scatter_dimension=0, tiled=True),
        lax.psum_scatter(grads[2], "fsdp", scatter_dimension=0, tiled=True),
        lax.psum_scatter(grads[3], "fsdp", scatter_dimension=0, tiled=True),
        lax.psum_scatter(grads[4], "fsdp", scatter_dimension=0, tiled=True),
        lax.psum_scatter(grads[5], "fsdp", scatter_dimension=0, tiled=True),
        lax.psum_scatter(grads[6], "fsdp", scatter_dimension=0, tiled=True),
        lax.psum_scatter(grads[7], "fsdp", scatter_dimension=0, tiled=True),
        lax.psum_scatter(grads[8], "fsdp", scatter_dimension=0, tiled=True),
    )
    return lax.psum(
        (
            shards[0],
            shards[1],
            shards[2],
            shards[3],
            shards[4],
            shards[5],
            shards[6],
            shards[7],
            shards[8],
        ),
        "dp",
    )


def on_device(
    latents,
    conditioning,
    seq_counts,
    cotangent,
    ada_weight,
    ada_bias,
    qkv_weight,
    proj_weight,
    proj_bias,
    up_weight,
    up_bias,
    down_weight,
    down_bias,
):
    stacks = (
        ada_weight,
        ada_bias,
        qkv_weight,
        proj_weight,
        proj_bias,
        up_weight,
        up_bias,
        down_weight,
        down_bias,
    )
    seq_slots = latents.shape[0]
    live = (jnp.arange(seq_slots, dtype=jnp.int32) < seq_counts[0]).astype(jnp.float32)[
        :, None, None
    ]
    inputs = []
    gathered = []
    current = latents
    for layer_idx in range(LAYERS):
        weights = gather_forward(stacks, layer_idx)
        gathered.append(weights)
        inputs.append(current)
        current = layer_parts(current, conditioning, weights)["result"]
    block_out = current * live
    grad = cotangent * live
    grad_cond = jnp.zeros(conditioning.shape, jnp.float32)
    layer_grads = [None] * LAYERS
    for layer_idx in reversed(range(LAYERS)):
        weights = gather_backward(stacks, layer_idx)
        grad, cond_part, grads = layer_backward(inputs[layer_idx], conditioning, weights, grad)
        grad_cond = grad_cond + cond_part
        layer_grads[layer_idx] = reduce_layer(grads)
    finals = [
        jnp.stack([layer_grads[layer_idx][piece_idx] for layer_idx in range(LAYERS)], axis=0)
        for piece_idx in range(9)
    ]
    return (
        block_out,
        grad,
        grad_cond,
        finals[0],
        finals[1],
        finals[2],
        finals[3],
        finals[4],
        finals[5],
        finals[6],
        finals[7],
        finals[8],
    )


def solution(mesh):
    in_specs = (
        P(("dp", "fsdp"), None, None),
        P(("dp", "fsdp"), None),
        P(("dp", "fsdp")),
        P(("dp", "fsdp"), None, None),
        P(None, "fsdp", None),
        P(None, "fsdp"),
        P(None, "fsdp", None),
        P(None, "fsdp", None),
        P(None, "fsdp"),
        P(None, "fsdp", None),
        P(None, "fsdp"),
        P(None, "fsdp", None),
        P(None, "fsdp"),
    )
    out_specs = (
        P(("dp", "fsdp"), None, None),
        P(("dp", "fsdp"), None, None),
        P(("dp", "fsdp"), None),
        P(None, "fsdp", None),
        P(None, "fsdp"),
        P(None, "fsdp", None),
        P(None, "fsdp", None),
        P(None, "fsdp"),
        P(None, "fsdp", None),
        P(None, "fsdp"),
        P(None, "fsdp", None),
        P(None, "fsdp"),
    )
    return jax.shard_map(
        on_device, mesh=mesh, in_specs=in_specs, out_specs=out_specs, check_vma=False
    )
```

profile of v0, /device:TPU:0, one launch (start us, length us, event | category | flops | bytes accessed | tf_op | source)
XLA Modules:
  0.0 733.3 jit_solution(9864900961176631379)
XLA Ops:
  17.1 6.2 all-gather.15
  23.9 5.7 all-gather.6
  31.0 11.7 %all-reduce.17 = (bf16[2304]{0:T(1024)(128)(2,1)S(1)}, bf16[384]{0:T(512)(128)(2,1)S(1)}, bf16[384]{0:T(512)(128)(2,1)S(1)}, bf16[2304]{0:T(1024)(128)(2,1)S(1)}...) all-reduce(bf16[2304]{0:T(1024)(128)(2,1)S(1)} %dynamic-update-slice, ...), channel_id=3, replica_groups=mesh['dp'=8,'fsdp'=4] {'fsdp'}, use_global_device_ids=true, to_apply=%add | all-reduce | flops 6144 | bytes 24576
  43.9 8.0 %all-gather.12 = bf16[1,384,384]{2,1,0:T(8,128)(2,1)} all-gather(bf16[1,96,384]{2,1,0:T(8,128)(2,1)S(1)} %get-tuple-element.91), channel_id=14, replica_groups=mesh['dp'=8,'fsdp'=4] {'fsdp'}, dimensions={1}, use_global_device_ids=true | all-gather | bytes 368640 | tf_op jit(solution)/shard_map/all_gather | solution.py:242
  51.9 7.2 all-gather.3
  59.1 9.7 %all-gather.11 = bf16[1,384,1152]{2,1,0:T(8,128)(2,1)} all-gather(bf16[1,96,1152]{2,1,0:T(8,128)(2,1)S(1)} %get-tuple-element.89), channel_id=13, replica_groups=mesh['dp'=8,'fsdp'=4] {'fsdp'}, dimensions={1}, use_global_device_ids=true | all-gather | bytes 1105920 | tf_op jit(solution)/shard_map/all_gather | solution.py:241
  68.8 13.9 %all-gather.2 = bf16[1,384,1152]{2,1,0:T(8,128)(2,1)S(1)} all-gather(bf16[1,96,1152]{2,1,0:T(8,128)(2,1)S(1)} %get-tuple-element.90), channel_id=4, replica_groups=mesh['dp'=8,'fsdp'=4] {'fsdp'}, dimensions={1}, use_global_device_ids=true | all-gather | bytes 1105920 | tf_op jit(solution)/shard_map/all_gather | solution.py:241
  87.5 2.4 convolution_convert_fusion.1
  89.9 2.7 copy.119
  93.4 3.6 fusion.146
  101.3 4.8 fusion.88
  106.1 5.7 fusion.135
  115.3 3.9 copy.125
  121.3 3.8 fusion.147
  131.4 5.0 fusion.82
  136.4 4.6 all-gather.35.cloned.1.call-done
  141.0 7.6 %fusion.148 = (f32[1536]{0:T(1024)}, bf16[3,256,1536]{2,1,0:T(8,128)(2,1)S(1)}) fusion(f32[3,256,1536]{2,1,0:T(8,128)} %fusion.82, f32[1536]{0:T(1024)} %convert_reduce_fusion, bf16[1,1536,384]{2,1,0:T(8,128)(2,1)} %all-gather.35.cloned.1.call-done, f32[3,256,384]{2,1,0:T(8,128)} %param.16, f32[3]{0:T(128)} %compare_convert_fusion, ...), kind=kOutput, calls=%fused_computation.256 | convolution fusion | flops 931625472 | bytes 9454092 | tf_op jit(solution)/shard_map/dot_general | solution.py:26
  152.6 4.5 multiply_reduce_fusion.23
  162.5 4.2 fusion.76
  166.7 4.1 fusion.112
  170.8 9.1 %fusion.67 = bf16[3,256,1,6,64]{1,4,3,0,2:T(8,128)(2,1)} fusion(f32[3,6,256,256]{2,3,1,0:T(8,128)} %fusion.112, bf16[3,256,3,6,64]{1,4,3,2,0:T(8,128)(2,1)} %bitcast.237, f32[3,6,256,256]{2,3,1,0:T(8,128)} %copy-done.18, f32[3,6,256]{2,1,0:T(8,128)} %copy-done.81), kind=kOutput, calls=%fused_computation.80 | convolution fusion | flops 159552256 | bytes 20103168 | tf_op jit(solution)/shard_map/shqk,skhd->sqhd/dot_general | solution.py:14
  179.8 8.9 %fusion.64 = bf16[3,256,1,6,64]{1,4,3,0,2:T(8,128)(2,1)} fusion(f32[3,6,256,256]{2,3,1,0:T(8,128)} %fusion.112, bf16[3,256,3,6,64]{1,4,3,2,0:T(8,128)(2,1)} %bitcast.238, f32[3,6,256,256]{2,3,1,0:T(8,128)} %copy-done.18, f32[3,6,256]{2,1,0:T(8,128)} %copy-done.81), kind=kOutput, calls=%fused_computation.79 | convolution fusion | flops 159552256 | bytes 20103168 | tf_op jit(solution)/shard_map/shqk,sqhd->skhd/dot_general | solution.py:14
  198.9 5.1 fusion.149
  212.0 4.4 convolution_bitcast_fusion.4
  216.6 2.5 convolution_convert_fusion.3
  221.2 4.2 fusion.110
  225.4 9.0 %fusion.73 = bf16[3,256,1,6,64]{1,4,3,0,2:T(8,128)(2,1)} fusion(f32[3,6,256,256]{2,3,1,0:T(8,128)} %fusion.110, bf16[3,256,3,6,64]{1,4,3,2,0:T(8,128)(2,1)} %bitcast.232, f32[3,6,256,256]{2,3,1,0:T(8,128)} %copy-done.17, f32[3,6,256]{2,1,0:T(8,128)} %copy-done.80), kind=kOutput, calls=%fused_computation.82 | convolution fusion | flops 159552256 | bytes 20103168 | tf_op jit(solution)/shard_map/shqk,skhd->sqhd/dot_general | solution.py:14
  234.4 9.0 %fusion.70 = bf16[3,256,1,6,64]{1,4,3,0,2:T(8,128)(2,1)} fusion(f32[3,6,256,256]{2,3,1,0:T(8,128)} %fusion.110, bf16[3,256,3,6,64]{1,4,3,2,0:T(8,128)(2,1)} %bitcast.233, f32[3,6,256,256]{2,3,1,0:T(8,128)} %copy-done.17, f32[3,6,256]{2,1,0:T(8,128)} %copy-done.80), kind=kOutput, calls=%fused_computation.81 | convolution fusion | flops 159552256 | bytes 20103168 | tf_op jit(solution)/shard_map/shqk,sqhd->skhd/dot_general | solution.py:14
  243.4 3.4 fusion.77
  248.5 2.5 convolution_bitcast_fusion.5
  251.1 6.5 convolution_bitcast_fusion
  257.7 4.4 convolution_bitcast_fusion.2
  263.3 6.3 convolution_bitcast_fusion.1
  270.4 4.4 convolution_bitcast_fusion.3
  279.5 3.8 multiply_reduce_fusion.7
  283.3 2.5 fusion.118
  286.0 16.1 %reduce-scatter.15.cloned.1.call-done = f32[96,1152]{1,0:T(8,128)} async-done(((f32[384,1152]{1,0:T(8,128)}), f32[96,1152]{1,0:T(8,128)}) %reduce-scatter.15.cloned.1.call-update) | async-done | bytes 442384 | tf_op jit(solution)/shard_map/reduce_scatter | solution.py:280
  302.0 35.4 %reduce-scatter.29.cloned.1.call-done = f32[384,384]{1,0:T(8,128)} async-done(((f32[1536,384]{1,0:T(8,128)}), f32[384,384]{1,0:T(8,128)}) %reduce-scatter.29.cloned.1.call-update) | async-done | bytes 589840 | tf_op jit(solution)/shard_map/reduce_scatter | solution.py:285
  337.4 35.2 %reduce-scatter.25.cloned.1.call-done = f32[96,1536]{1,0:T(8,128)} async-done(((f32[384,1536]{1,0:T(8,128)}), f32[96,1536]{1,0:T(8,128)}) %reduce-scatter.25.cloned.1.call-update) | async-done | bytes 589840 | tf_op jit(solution)/shard_map/reduce_scatter | solution.py:283
  372.6 35.4 %reduce-scatter.27.cloned.1.call-done = f32[384,384]{1,0:T(8,128)} async-done(((f32[1536,384]{1,0:T(8,128)}), f32[384,384]{1,0:T(8,128)}) %reduce-scatter.27.cloned.1.call-update) | async-done | bytes 589840 | tf_op jit(solution)/shard_map/reduce_scatter | solution.py:285
  408.0 35.2 %reduce-scatter.23.cloned.1.call-done = f32[96,1536]{1,0:T(8,128)} async-done(((f32[384,1536]{1,0:T(8,128)}), f32[96,1536]{1,0:T(8,128)}) %reduce-scatter.23.cloned.1.call-update) | async-done | bytes 589840 | tf_op jit(solution)/shard_map/reduce_scatter | solution.py:283
  443.3 42.8 %reduce-scatter.13.cloned.1.call-done = f32[96,2304]{1,0:T(8,128)} async-done(((f32[384,2304]{1,0:T(8,128)}), f32[96,2304]{1,0:T(8,128)}) %reduce-scatter.13.cloned.1.call-update) | async-done | bytes 884752 | tf_op jit(solution)/shard_map/reduce_scatter | solution.py:278
  486.1 42.8 %reduce-scatter.11.cloned.1.call-done = f32[96,2304]{1,0:T(8,128)} async-done(((f32[384,2304]{1,0:T(8,128)}), f32[96,2304]{1,0:T(8,128)}) %reduce-scatter.11.cloned.1.call-update) | async-done | bytes 884752 | tf_op jit(solution)/shard_map/reduce_scatter | solution.py:278
  531.2 10.6 %all-reduce.16 = (f32[2304]{0:T(1024)S(1)}, f32[2304]{0:T(1024)S(1)}, f32[384]{0:T(512)S(1)}, f32[384]{0:T(512)S(1)}, f32[1536]{0:T(1024)S(1)}, /*index=5*/f32[1536]{0:T(1024)S(1)}, f32[384]{0:T(512)S(1)}, f32[384]{0:T(512)S(1)}) all-reduce(f32[2304]{0:T(1024)S(1)} %reduce_sum.433, ...), channel_id=23, replica_groups=mesh['dp'=8,'fsdp'=4] {'fsdp'}, use_global_device_ids=true, to_apply=%region_42.43.clone | all-reduce | flops 9216 | bytes 73728
  542.4 39.5 %all-reduce.14 = (f32[1,576]{1,0:T(1,128)S(1)}, f32[1,576]{1,0:T(1,128)S(1)}, f32[1,96]{1,0:T(1,128)S(1)}, f32[1,96]{1,0:T(1,128)S(1)}, f32[1,384]{1,0:T(1,128)S...) all-reduce(f32[1,576]{1,0:T(1,128)S(1)} %stack.125, ...), channel_id=1, replica_groups=mesh['dp'=8,'fsdp'=4] {'dp'}, use_global_device_ids=true, to_apply=%region_43.44 | all-reduce | flops 2304 | bytes 18432 | tf_op jit(solution)/shard_map/psum | solution.py:288
  587.6 2.8 multiply_add_fusion.2
  590.4 129.4 %all-reduce.20.cloned.1.call-done = (f32[1,96,2304]{2,1,0:T(8,128)}, f32[1,96,2304]{2,1,0:T(8,128)}, f32[1,96,1152]{2,1,0:T(8,128)}, f32[1,96,1152]{2,1,0:T(8,12...) async-done(((f32[1,96,2304]{2,1,0:T(8,128)}, ...) | async-done | bytes 5308432 | tf_op jit(solution)/shard_map/psum | solution.py:288
  719.8 2.8 pad_maximum_fusion.2
  (404 shorter events, 80.6 us)
Async XLA Ops:
  7.2 75.5 %all-gather.25.cloned.1.call-start = ((), (), s32[]{:S(2)}) async-start(), calls=%async_computation.20 | async-start | bytes 2211840 | tf_op jit(solution)/shard_map/all_gather | solution.py:239
  9.5 75.5 %all-gather.31.cloned.1.call-start = ((), (), s32[]{:S(2)}) async-start(), calls=%async_computation.23 | async-start | bytes 2211840 | tf_op jit(solution)/shard_map/all_gather | solution.py:239
  10.2 6.2 copy-start.113
  10.2 6.2 copy-start.114
  10.3 6.2 copy-start.108
  10.3 6.3 copy-start
  10.3 91.0 %all-gather.27.cloned.1.call-start = ((), (), s32[]{:S(2)}) async-start(), calls=%async_computation.21 | async-start | bytes 1474560 | tf_op jit(solution)/shard_map/all_gather | solution.py:244
  11.2 94.9 %all-gather.29.cloned.1.call-start = ((), (), s32[]{:S(2)}) async-start(), calls=%async_computation.22 | async-start | bytes 1474560 | tf_op jit(solution)/shard_map/all_gather | solution.py:246
  12.1 31.7 %copy-start.52 = (bf16[2,96,384]{2,1,0:T(8,128)(2,1)S(1)}, bf16[2,96,384]{2,1,0:T(8,128)(2,1)}, u32[]{:S(2)}) copy-start(bf16[2,96,384]{2,1,0:T(8,128)(2,1)} %param.20) | copy-start | bytes 442372
  12.2 119.2 %all-gather.33.cloned.1.call-start = ((), (), s32[]{:S(2)}) async-start(), calls=%async_computation.24 | async-start | bytes 1474560 | tf_op jit(solution)/shard_map/all_gather | solution.py:244
  12.8 128.2 %all-gather.35.cloned.1.call-start = ((), (), s32[]{:S(2)}) async-start(), calls=%async_computation.25 | async-start | bytes 1474560 | tf_op jit(solution)/shard_map/all_gather | solution.py:246
  13.3 272.6 %reduce-scatter.21.cloned.1.call-start = ((), (), s32[]{:S(2)}) async-start(), calls=%async_computation.15 | async-start | bytes 737280 | tf_op jit(solution)/shard_map/reduce_scatter | solution.py:281
  16.5 42.6 %copy-start.48 = (bf16[2,96,1152]{2,1,0:T(8,128)(2,1)S(1)}, bf16[2,96,1152]{2,1,0:T(8,128)(2,1)}, u32[]{:S(2)}) copy-start(bf16[2,96,1152]{2,1,0:T(8,128)(2,1)} %param.19) | copy-start | bytes 1327108
  16.7 70.7 %copy-start.66 = (f32[3,256]{1,0:T(4,128)}, f32[3,256]{1,0:T(4,128)S(1)}, u32[]{:S(2)}) copy-start(f32[3,256]{1,0:T(4,128)S(1)} %broadcast_multiply_fusion.11) | copy-start | bytes 9220
  17.1 70.4 %copy-start.82 = (f32[3,256]{1,0:T(4,128)}, f32[3,256]{1,0:T(4,128)S(1)}, u32[]{:S(2)}) copy-start(f32[3,256]{1,0:T(4,128)S(1)} %add_rsqrt_fusion.3) | copy-start | bytes 9220
  29.6 76.5 %copy-start.91 = (f32[1536]{0:T(1024)}, f32[1536]{0:T(1024)S(1)}, u32[]{:S(2)}) copy-start(f32[1536]{0:T(1024)S(1)} %convert_reduce_fusion.1) | copy-start | bytes 18436
  51.9 30.9 %copy-start.49 = (f32[3,384]{1,0:T(4,128)S(1)}, f32[3,384]{1,0:T(4,128)}, u32[]{:S(2)}) copy-start(f32[3,384]{1,0:T(4,128)} %param.14) | copy-start | bytes 13828
  59.1 40.1 %copy-start.19 = (bf16[1,384,384]{2,1,0:T(8,128)(2,1)}, bf16[1,384,384]{2,1,0:T(8,128)(2,1)S(1)}, u32[]{:S(2)}) copy-start(bf16[1,384,384]{2,1,0:T(8,128)(2,1)S(1)} %all-gather.3) | copy-start | bytes 884740
  84.9 14.3 %copy-start.59 = (f32[3,384]{1,0:T(4,128)}, f32[3,384]{1,0:T(4,128)S(1)}, u32[]{:S(2)}) copy-start(f32[3,384]{1,0:T(4,128)S(1)} %get-tuple-element.104) | copy-start | bytes 13828
  84.9 16.3 %copy-start.56 = (f32[3,384]{1,0:T(4,128)}, f32[3,384]{1,0:T(4,128)S(1)}, u32[]{:S(2)}) copy-start(f32[3,384]{1,0:T(4,128)S(1)} %get-tuple-element.101) | copy-start | bytes 13828
  84.9 16.3 %copy-start.61 = (f32[3,384]{1,0:T(4,128)}, f32[3,384]{1,0:T(4,128)S(1)}, u32[]{:S(2)}) copy-start(f32[3,384]{1,0:T(4,128)S(1)} %get-tuple-element.100) | copy-start | bytes 13828
  84.9 21.2 %copy-start.74 = (f32[3,384]{1,0:T(4,128)}, f32[3,384]{1,0:T(4,128)S(1)}, u32[]{:S(2)}) copy-start(f32[3,384]{1,0:T(4,128)S(1)} %get-tuple-element.99) | copy-start | bytes 13828
  87.4 24.8 %copy-start.76 = (f32[3,384]{1,0:T(4,128)}, f32[3,384]{1,0:T(4,128)S(1)}, u32[]{:S(2)}) copy-start(f32[3,384]{1,0:T(4,128)S(1)} %get-tuple-element.97) | copy-start | bytes 13828
  87.4 24.8 %copy-start.99 = (f32[3,384]{1,0:T(4,128)}, f32[3,384]{1,0:T(4,128)S(1)}, u32[]{:S(2)}) copy-start(f32[3,384]{1,0:T(4,128)S(1)} %get-tuple-element.96) | copy-start | bytes 13828
  106.1 6.8 copy-start.36
  141.0 7.6 %copy-start.34 = (bf16[1,384,1536]{2,1,0:T(8,128)(2,1)S(1)}, bf16[1,384,1536]{2,1,0:T(8,128)(2,1)}, u32[]{:S(2)}) copy-start(bf16[1,384,1536]{2,1,0:T(8,128)(2,1)} %all-gather.33.cloned.1.call-done) | copy-start | bytes 3538948
  141.0 7.6 %copy-start.51 = (f32[3,256]{1,0:T(4,128)S(1)}, f32[3,256]{1,0:T(4,128)}, u32[]{:S(2)}) copy-start(f32[3,256]{1,0:T(4,128)} %copy-done.50) | copy-start | bytes 9220
  141.0 7.6 %copy-start.55 = (f32[3,256]{1,0:T(4,128)S(1)}, f32[3,256]{1,0:T(4,128)}, u32[]{:S(2)}) copy-start(f32[3,256]{1,0:T(4,128)} %add_rsqrt_fusion) | copy-start | bytes 9220
  141.0 7.6 %copy-start.63 = (f32[3,384]{1,0:T(4,128)S(1)}, f32[3,384]{1,0:T(4,128)}, u32[]{:S(2)}) copy-start(f32[3,384]{1,0:T(4,128)} %get-tuple-element.95) | copy-start | bytes 13828
  141.0 9.9 %copy-start.117 = (bf16[1,1536,384]{2,1,0:T(8,128)(2,1)S(1)}, bf16[1,1536,384]{2,1,0:T(8,128)(2,1)}, u32[]{:S(2)}) copy-start(bf16[1,1536,384]{2,1,0:T(8,128)(2,1)} %all-gather.35.cloned.1.call-done) | copy-start | bytes 3538948
  191.9 94.1 %reduce-scatter.19.cloned.1.call-start = ((), (), s32[]{:S(2)}) async-start(), calls=%async_computation.14 | async-start | bytes 737280 | tf_op jit(solution)/shard_map/reduce_scatter | solution.py:281
  193.7 5.2 slice-start
  198.8 8.0 %copy-start.12 = (f32[3,256,384]{2,1,0:T(8,128)}, f32[3,256,384]{2,1,0:T(8,128)S(1)}, u32[]{:S(2)}) copy-start(f32[3,256,384]{2,1,0:T(8,128)S(1)} %get-tuple-element.70) | copy-start | bytes 3538948
  198.9 5.1 copy-start.57
  211.9 74.0 %reduce-scatter.17.cloned.1.call-start = ((), (), s32[]{:S(2)}) async-start(), calls=%async_computation.13 | async-start | bytes 2211840 | tf_op jit(solution)/shard_map/reduce_scatter | solution.py:280
  216.4 85.7 %reduce-scatter.15.cloned.1.call-start = ((), (), s32[]{:S(2)}) async-start(), calls=%async_computation.12 | async-start | bytes 2211840 | tf_op jit(solution)/shard_map/reduce_scatter | solution.py:280
  251.1 86.3 %reduce-scatter.29.cloned.1.call-start = ((), (), s32[]{:S(2)}) async-start(), calls=%async_computation.19 | async-start | bytes 2949120 | tf_op jit(solution)/shard_map/reduce_scatter | solution.py:285
  257.6 115.0 %reduce-scatter.25.cloned.1.call-start = ((), (), s32[]{:S(2)}) async-start(), calls=%async_computation.17 | async-start | bytes 2949120 | tf_op jit(solution)/shard_map/reduce_scatter | solution.py:283
  262.1 145.9 %reduce-scatter.27.cloned.1.call-start = ((), (), s32[]{:S(2)}) async-start(), calls=%async_computation.18 | async-start | bytes 2949120 | tf_op jit(solution)/shard_map/reduce_scatter | solution.py:285
  269.7 173.6 %reduce-scatter.23.cloned.1.call-start = ((), (), s32[]{:S(2)}) async-start(), calls=%async_computation.16 | async-start | bytes 2949120 | tf_op jit(solution)/shard_map/reduce_scatter | solution.py:283
  274.8 211.3 %reduce-scatter.13.cloned.1.call-start = ((), (), s32[]{:S(2)}) async-start(), calls=%async_computation.11 | async-start | bytes 4423680 | tf_op jit(solution)/shard_map/reduce_scatter | solution.py:278
  278.0 5.2 copy-start.79
  278.0 5.3 copy-start.105
  278.0 5.3 copy-start.104
  278.0 5.3 copy-start.78
  278.0 250.9 %reduce-scatter.11.cloned.1.call-start = ((), (), s32[]{:S(2)}) async-start(), calls=%async_computation.10 | async-start | bytes 4423680 | tf_op jit(solution)/shard_map/reduce_scatter | solution.py:278
  285.9 434.0 %all-reduce.20.cloned.1.call-start = ((), (), s32[]{:S(2)}) async-start(), calls=%async_computation.26 | async-start | bytes 10616832 | tf_op jit(solution)/shard_map/psum | solution.py:288
  529.0 57.4 %copy-start.7 = (bf16[1,384,2304]{2,1,0:T(8,128)(2,1)S(1)}, bf16[1,384,2304]{2,1,0:T(8,128)(2,1)}, u32[]{:S(2)}) copy-start(bf16[1,384,2304]{2,1,0:T(8,128)(2,1)} %all-gather.25.cloned.1.call-done) | copy-start | bytes 5308420
  (90 other events, 213.6 us)
Sparse Core Ops, SparseCore 0:
  10.1 23.4 all-gather.24
  35.8 23.4 all-gather.30
  61.5 21.6 all-gather.26
  85.1 17.4 all-gather.28
  104.0 17.4 all-gather.32
  123.5 17.4 all-gather.34
  192.0 22.0 reduce-scatter.20
  216.5 22.0 reduce-scatter.18
  241.2 29.1 reduce-scatter.16
  272.8 29.1 reduce-scatter.14
  304.6 32.7 reduce-scatter.28
  339.8 32.8 reduce-scatter.24
  375.2 32.8 reduce-scatter.26
  410.4 32.8 reduce-scatter.22
  445.7 40.3 reduce-scatter.12
  488.5 40.3 reduce-scatter.10
  533.5 186.2 all-reduce.19
where the time goes:
time: 738 us; the launch traced here: 733 us
  waiting for transfers between devices  379 us (51%)
  matrix products  156 us (21%)
  blocking collectives  112 us (15%)
  local copies, waits for them, and re-layouts  36.4 us (5%)
  other arithmetic  29 us (4%)
  between operations  19.4 us (3%)
    psum x1, waiting for transfers between devices, reduce_layer(): lax.psum((shards[0], shards[1], shards[2], shards[3], shards[4], shards[5...  129 us
    reduce_scatter x2, waiting for transfers between devices, reduce_layer(): lax.psum_scatter(grads[0], 'fsdp', scatter_dimension=0, tiled=True)  85.7 us
    reduce_scatter x2, waiting for transfers between devices, reduce_layer(): lax.psum_scatter(grads[7], 'fsdp', scatter_dimension=0, tiled=True)  70.7 us
    reduce_scatter x2, waiting for transfers between devices, reduce_layer(): lax.psum_scatter(grads[5], 'fsdp', scatter_dimension=0, tiled=True)  70.5 us
    dot_general x12, matrix products, einsum_mixed(): return jnp.einsum(form, left, right, preferred_element_type=jnp.float32)  57.6 us
    psum x1, blocking collectives, reduce_layer(): lax.psum((shards[0], shards[1], shards[2], shards[3], shards[4], shards[5...  39.5 us
    dot_general x8, matrix products, outer_total(): jnp.dot(left.reshape(-1, left.shape[-1]).T, right.reshape(-1, right.shape...  31.1 us
    dot_general x8, matrix products, matmul_last(): jnp.dot(flat, right, preferred_element_type=jnp.float32)  28.3 us
  transfers between devices with their start and end apart: 17, of which 9 were waited for; matrix products, arithmetic and copies ran while one was open for 20% of the time, Pallas kernels for 0%

commit v1 on v0

--- a/solution.py
+++ b/solution.py
@@ -8,6 +8,28 @@
 NORM_EPS = 1e-06
 GELU_K = 0.7978845608028654
 GELU_C = 0.044715
+
+
+def laid_out(tiles, dim):
+    lengths = list(tiles.shape[1:])
+    lengths[dim] *= tiles.shape[0]
+    return jnp.moveaxis(tiles, 0, dim).reshape(lengths)
+
+
+def doubled(shard, axis):
+    size = lax.axis_size(axis)
+    blocks = shard[None]
+    for level in range(size.bit_length() - 1):
+        bit = 1 << level
+        other = lax.ppermute(blocks, axis, [(i, i ^ bit) for i in range(size)])
+        both = jnp.stack([blocks, other])
+        upper = lax.axis_index(axis) >> level & 1
+        blocks = jnp.where(upper == 0, both, both[::-1]).reshape(-1, *shard.shape)
+    return blocks
+
+
+def doubled_up(array, axis, dim):
+    return laid_out(doubled(array, axis), dim)
 
 
 def einsum_mixed(form, left, right):
@@ -238,7 +260,7 @@
     return (
         lax.all_gather(ada_weight[layer_idx], "fsdp", axis=0, tiled=True),
         lax.all_gather(ada_bias[layer_idx], "fsdp", axis=0, tiled=True),
-        lax.all_gather(qkv_weight[layer_idx], "fsdp", axis=0, tiled=True),
+        doubled_up(qkv_weight[layer_idx], "fsdp", 0),
         lax.all_gather(proj_weight[layer_idx], "fsdp", axis=0, tiled=True),
         lax.all_gather(proj_bias[layer_idx], "fsdp", axis=0, tiled=True),
         lax.all_gather(up_weight[layer_idx], "fsdp", axis=0, tiled=True),

time: 738 us -> 764 us (1.035)
  waiting for transfers between devices: 379 us -> 338 us
  matrix products: 156 us -> 179 us
  other arithmetic: 29 us -> 46.3 us
  blocking collectives: 112 us -> 126 us
  local copies, waits for them, and re-layouts: 36.4 us -> 46.1 us
    reduce_scatter x2, waiting for transfers between devices: 70.5 us -> 43.2 us  [reduce_layer(): lax.psum_scatter(grads[5], 'fsdp', scatter_dimension=0, tiled=True)]
    reduce_scatter x2, waiting for transfers between devices: 16.1 us -> 0.01 us  [reduce_layer(): lax.psum_scatter(grads[2], 'fsdp', scatter_dimension=0, tiled=True)]
    dot_general x8 -> x14, matrix products: 28.3 us -> 42.5 us  [matmul_last(): jnp.dot(flat, right, preferred_element_type=jnp.float32)]
    all_gather x2, blocking collectives: 15.2 us -> 27.8 us  [gather_forward(): lax.all_gather(proj_weight[layer_idx], 'fsdp', axis=0, tiled=True)]
    dot_general x12 -> x16, matrix products: 57.6 us -> 68.2 us  [einsum_mixed(): return jnp.einsum(form, left, right, preferred_element_type=jnp.float32)]
    ppermute x0 -> x4, waiting for transfers between devices: none -> 10.6 us  [doubled(): other = lax.ppermute(blocks, axis, [(i, i ^ bit) for i in range(size)])]
    convert_element_type x2 -> x4, local copies, waits for them, and re-layouts: 6.52 us -> 15.4 us  [layer_parts(): qkv = matmul_last(attn_in, qkv_weight).astype(jnp.bfloat16)]
    unnamed x273 -> x293, local copies, waits for them, and re-layouts: 18.8 us -> 21.8 us
  transfers between devices with their start and end apart: 17 -> 21, of which waited for: 9 -> 9; matrix products, arithmetic and copies ran while one was open for 20% -> 24% of each run, Pallas kernels for 0% -> 0%
where the time goes in v1:
time: 764 us; the launch traced here: 758 us
  waiting for transfers between devices  338 us (44%)
  matrix products  179 us (23%)
  blocking collectives  126 us (16%)
  other arithmetic  46.3 us (6%)
  local copies, waits for them, and re-layouts  46.1 us (6%)
  between operations  19.4 us (3%)
    psum x1, waiting for transfers between devices, reduce_layer(): lax.psum((shards[0], shards[1], shards[2], shards[3], shards[4], shards[5...  126 us
    reduce_scatter x2, waiting for transfers between devices, reduce_layer(): lax.psum_scatter(grads[0], 'fsdp', scatter_dimension=0, tiled=True)  85.7 us
    reduce_scatter x2, waiting for transfers between devices, reduce_layer(): lax.psum_scatter(grads[7], 'fsdp', scatter_dimension=0, tiled=True)  70.6 us
    dot_general x16, matrix products, einsum_mixed(): return jnp.einsum(form, left, right, preferred_element_type=jnp.float32)  68.2 us
    reduce_scatter x2, waiting for transfers between devices, reduce_layer(): lax.psum_scatter(grads[5], 'fsdp', scatter_dimension=0, tiled=True)  43.2 us
    dot_general x14, matrix products, matmul_last(): jnp.dot(flat, right, preferred_element_type=jnp.float32)  42.5 us
    psum x1, blocking collectives, reduce_layer(): lax.psum((shards[0], shards[1], shards[2], shards[3], shards[4], shards[5...  40 us
    dot_general x8, matrix products, outer_total(): jnp.dot(left.reshape(-1, left.shape[-1]).T, right.reshape(-1, right.shape...  30.5 us
  transfers between devices with their start and end apart: 21, of which 9 were waited for; matrix products, arithmetic and copies ran while one was open for 24% of the time, Pallas kernels for 0%

profile of v1, /device:TPU:0, one launch (start us, length us, event | category | flops | bytes accessed | tf_op | source)
XLA Modules:
  0.0 758.5 jit_solution(4989654449993111503)
XLA Ops:
  14.1 12.3 %all-gather.17 = bf16[1,384,1152]{2,1,0:T(8,128)(2,1)} all-gather(bf16[1,96,1152]{2,1,0:T(8,128)(2,1)S(1)} %get-tuple-element.86), channel_id=19, replica_groups=mesh['dp'=8,'fsdp'=4] {'fsdp'}, dimensions={1}, use_global_device_ids=true | all-gather | bytes 1105920 | tf_op jit(solution)/shard_map/all_gather | solution.py:288
  29.7 13.5 %all-reduce.17 = (bf16[2304]{0:T(1024)(128)(2,1)S(1)}, bf16[384]{0:T(512)(128)(2,1)S(1)}, bf16[384]{0:T(512)(128)(2,1)S(1)}, bf16[2304]{0:T(1024)(128)(2,1)S(1)}...) all-reduce(bf16[2304]{0:T(1024)(128)(2,1)S(1)} %dynamic-update-slice, ...), channel_id=3, replica_groups=mesh['dp'=8,'fsdp'=4] {'fsdp'}, use_global_device_ids=true, to_apply=%add | all-reduce | flops 6144 | bytes 24576
  44.4 7.2 all-gather.2
  52.2 5.3 all-gather.5
  59.4 5.2 all-gather.13
  67.6 20.6 %all-gather.10 = bf16[1,384,384]{2,1,0:T(8,128)(2,1)} all-gather(bf16[1,96,384]{2,1,0:T(8,128)(2,1)S(1)} %get-tuple-element.89), channel_id=12, replica_groups=mesh['dp'=8,'fsdp'=4] {'fsdp'}, dimensions={1}, use_global_device_ids=true | all-gather | bytes 368640 | tf_op jit(solution)/shard_map/all_gather | solution.py:264
  88.2 9.9 %all-gather.16 = bf16[1,384,1152]{2,1,0:T(8,128)(2,1)} all-gather(bf16[1,96,1152]{2,1,0:T(8,128)(2,1)S(1)} %get-tuple-element.85), channel_id=18, replica_groups=mesh['dp'=8,'fsdp'=4] {'fsdp'}, dimensions={1}, use_global_device_ids=true | all-gather | bytes 1105920 | tf_op jit(solution)/shard_map/all_gather | solution.py:288
  103.9 3.9 copy.160
  109.8 3.6 fusion.221
  119.3 5.1 fusion.223
  130.2 3.8 copy.173
  136.2 3.9 fusion.229
  144.4 4.9 fusion.120
  149.3 7.5 fusion.230
  163.6 4.0 fusion.113
  167.6 4.1 fusion.171
  171.7 9.0 %fusion.101 = bf16[3,256,1,6,64]{1,4,3,0,2:T(8,128)(2,1)} fusion(f32[3,6,256,256]{2,3,1,0:T(8,128)} %fusion.171, bf16[3,256,3,6,64]{1,4,3,2,0:T(8,128)(2,1)} %bitcast.333, f32[3,6,256,256]{2,3,1,0:T(8,128)} %copy-done.21, f32[3,6,256]{2,1,0:T(8,128)S(1)} %copy-done.98), kind=kOutput, calls=%fused_computation.128 | convolution fusion | flops 159552256 | bytes 20103168 | tf_op jit(solution)/shard_map/shqk,sqhd->skhd/dot_general | solution.py:36
  180.7 9.0 %fusion.104 = bf16[3,256,1,6,64]{1,4,3,0,2:T(8,128)(2,1)} fusion(f32[3,6,256,256]{2,3,1,0:T(8,128)} %fusion.171, bf16[3,256,3,6,64]{1,4,3,2,0:T(8,128)(2,1)} %bitcast.334, f32[3,6,256,256]{2,3,1,0:T(8,128)} %copy-done.21, f32[3,6,256]{2,1,0:T(8,128)S(1)} %copy-done.98), kind=kOutput, calls=%fused_computation.129 | convolution fusion | flops 159552256 | bytes 20103168 | tf_op jit(solution)/shard_map/shqk,skhd->sqhd/dot_general | solution.py:36
  189.7 3.4 convolution_convert_fusion
  193.1 3.8 copy.185
  199.0 3.6 fusion.228
  220.8 4.6 fusion.231
  233.3 3.8 convolution_bitcast_fusion.4
  242.1 4.2 fusion.173
  246.3 9.2 %fusion.107 = bf16[3,256,1,6,64]{1,4,3,0,2:T(8,128)(2,1)} fusion(f32[3,6,256,256]{2,3,1,0:T(8,128)} %fusion.173, bf16[3,256,3,6,64]{1,4,3,2,0:T(8,128)(2,1)} %bitcast.328, f32[3,6,256,256]{2,3,1,0:T(8,128)} %copy-done.20, f32[3,6,256]{2,1,0:T(8,128)} %copy-done.96), kind=kOutput, calls=%fused_computation.130 | convolution fusion | flops 159552256 | bytes 20103168 | tf_op jit(solution)/shard_map/shqk,sqhd->skhd/dot_general | solution.py:36
  255.4 9.3 %fusion.110 = bf16[3,256,1,6,64]{1,4,3,0,2:T(8,128)(2,1)} fusion(f32[3,6,256,256]{2,3,1,0:T(8,128)} %fusion.173, bf16[3,256,3,6,64]{1,4,3,2,0:T(8,128)(2,1)} %bitcast.329, f32[3,6,256,256]{2,3,1,0:T(8,128)} %copy-done.20, f32[3,6,256]{2,1,0:T(8,128)} %copy-done.96), kind=kOutput, calls=%fused_computation.131 | convolution fusion | flops 159552256 | bytes 20103168 | tf_op jit(solution)/shard_map/shqk,skhd->sqhd/dot_general | solution.py:36
  264.7 3.4 fusion.114
  272.8 5.0 convolution_bitcast_fusion.2
  278.5 4.4 convolution_bitcast_fusion.3
  284.1 6.0 convolution_bitcast_fusion
  291.5 6.3 convolution_bitcast_fusion.1
  301.4 5.3 fusion.99
  310.4 4.9 multiply_reduce_fusion.8
  315.4 4.3 fusion.100
  329.3 9.4 %collective-permute-done.3 = bf16[2,96,1152]{2,1,0:T(8,128)(2,1)S(1)} collective-permute-done((bf16[2,96,1152]{2,1,0:T(8,128)(2,1)}, bf16[2,96,1152]{2,1,0:T(8,128)(2,1)S(1)}, u32[]{:S(2)}, u32[]{:S(2)}) %collective-permute-start.3) | collective-permute-done | bytes 442400 | tf_op jit(solution)/shard_map/ppermute | solution.py:24
  339.6 11.5 %all-reduce.16 = (f32[2304]{0:T(1024)S(1)}, f32[2304]{0:T(1024)S(1)}, f32[384]{0:T(512)S(1)}, f32[384]{0:T(512)S(1)}, f32[1536]{0:T(1024)S(1)}, /*index=5*/f32[1536]{0:T(1024)S(1)}, f32[384]{0:T(512)S(1)}, f32[384]{0:T(512)S(1)}) all-reduce(f32[2304]{0:T(1024)S(1)} %reduce_sum.469, ...), channel_id=23, replica_groups=mesh['dp'=8,'fsdp'=4] {'fsdp'}, use_global_device_ids=true, to_apply=%region_50.51.clone | all-reduce | flops 9216 | bytes 73728
  351.1 3.4 convolution_convert_fusion.2
  354.6 8.0 %reduce-scatter.25.cloned.1.call-done = f32[96,1536]{1,0:T(8,128)} async-done(((f32[384,1536]{1,0:T(8,128)}), f32[96,1536]{1,0:T(8,128)}) %reduce-scatter.25.cloned.1.call-update) | async-done | bytes 589840 | tf_op jit(solution)/shard_map/reduce_scatter | solution.py:305
  362.6 35.2 %reduce-scatter.23.cloned.1.call-done = f32[96,1536]{1,0:T(8,128)} async-done(((f32[384,1536]{1,0:T(8,128)}), f32[96,1536]{1,0:T(8,128)}) %reduce-scatter.23.cloned.1.call-update) | async-done | bytes 589840 | tf_op jit(solution)/shard_map/reduce_scatter | solution.py:305
  397.8 35.4 %reduce-scatter.29.cloned.1.call-done = f32[384,384]{1,0:T(8,128)} async-done(((f32[1536,384]{1,0:T(8,128)}), f32[384,384]{1,0:T(8,128)}) %reduce-scatter.29.cloned.1.call-update) | async-done | bytes 589840 | tf_op jit(solution)/shard_map/reduce_scatter | solution.py:307
  433.2 35.2 %reduce-scatter.27.cloned.1.call-done = f32[384,384]{1,0:T(8,128)} async-done(((f32[1536,384]{1,0:T(8,128)}), f32[384,384]{1,0:T(8,128)}) %reduce-scatter.27.cloned.1.call-update) | async-done | bytes 589840 | tf_op jit(solution)/shard_map/reduce_scatter | solution.py:307
  468.4 42.8 %reduce-scatter.13.cloned.1.call-done = f32[96,2304]{1,0:T(8,128)} async-done(((f32[384,2304]{1,0:T(8,128)}), f32[96,2304]{1,0:T(8,128)}) %reduce-scatter.13.cloned.1.call-update) | async-done | bytes 884752 | tf_op jit(solution)/shard_map/reduce_scatter | solution.py:300
  511.2 42.8 %reduce-scatter.11.cloned.1.call-done = f32[96,2304]{1,0:T(8,128)} async-done(((f32[384,2304]{1,0:T(8,128)}), f32[96,2304]{1,0:T(8,128)}) %reduce-scatter.11.cloned.1.call-update) | async-done | bytes 884752 | tf_op jit(solution)/shard_map/reduce_scatter | solution.py:300
  554.2 3.9 copy.167
  558.6 40.0 %all-reduce.14 = (f32[1,576]{1,0:T(1,128)S(1)}, f32[1,576]{1,0:T(1,128)S(1)}, f32[1,96]{1,0:T(1,128)S(1)}, f32[1,96]{1,0:T(1,128)S(1)}, f32[1,384]{1,0:T(1,128)S...) all-reduce(f32[1,576]{1,0:T(1,128)S(1)} %stack.157, ...), channel_id=1, replica_groups=mesh['dp'=8,'fsdp'=4] {'dp'}, use_global_device_ids=true, to_apply=%region_51.52 | all-reduce | flops 2304 | bytes 18432 | tf_op jit(solution)/shard_map/psum | solution.py:310
  603.0 3.6 fusion.226
  613.5 5.4 fusion.82
  618.8 126.1 %all-reduce.20.cloned.1.call-done = (f32[1,96,2304]{2,1,0:T(8,128)}, f32[1,96,2304]{2,1,0:T(8,128)}, f32[1,96,1152]{2,1,0:T(8,128)}, f32[1,96,1152]{2,1,0:T(8,12...) async-done(((f32[1,96,2304]{2,1,0:T(8,128)}, ...) | async-done | bytes 5308432 | tf_op jit(solution)/shard_map/psum | solution.py:310
  (462 shorter events, 121.8 us)
Async XLA Ops:
  7.2 91.2 %all-gather.25.cloned.1.call-start = ((), (), s32[]{:S(2)}) async-start(), calls=%async_computation.20 | async-start | bytes 2211840 | tf_op jit(solution)/shard_map/all_gather | solution.py:261
  9.5 107.3 %all-gather.31.cloned.1.call-start = ((), (), s32[]{:S(2)}) async-start(), calls=%async_computation.23 | async-start | bytes 2211840 | tf_op jit(solution)/shard_map/all_gather | solution.py:261
  10.2 109.0 %all-gather.29.cloned.1.call-start = ((), (), s32[]{:S(2)}) async-start(), calls=%async_computation.22 | async-start | bytes 1474560 | tf_op jit(solution)/shard_map/all_gather | solution.py:268
  11.2 108.1 %all-gather.27.cloned.1.call-start = ((), (), s32[]{:S(2)}) async-start(), calls=%async_computation.21 | async-start | bytes 1474560 | tf_op jit(solution)/shard_map/all_gather | solution.py:266
  12.1 14.3 %copy-start.108 = (bf16[2,576]{1,0:T(2,128)(2,1)S(1)}, bf16[2,576]{1,0:T(2,128)(2,1)}, u32[]{:S(2)}) copy-start(bf16[2,576]{1,0:T(2,128)(2,1)} %param.18) | copy-start | bytes 6916
  12.1 14.3 %copy-start.126 = (bf16[2,96]{1,0:T(2,128)(2,1)S(1)}, bf16[2,96]{1,0:T(2,128)(2,1)}, u32[]{:S(2)}) copy-start(bf16[2,96]{1,0:T(2,128)(2,1)} %param.21) | copy-start | bytes 1156
  12.1 14.4 %copy-start.123 = (u32[32]{0:T(128)S(1)}, u32[32]{0:T(128)}, u32[]{:S(2)}) copy-start(u32[32]{0:T(128)} %constant.61) | copy-start | bytes 388
  12.1 16.3 %copy-start.127 = (bf16[2,96]{1,0:T(2,128)(2,1)S(1)}, bf16[2,96]{1,0:T(2,128)(2,1)}, u32[]{:S(2)}) copy-start(bf16[2,96]{1,0:T(2,128)(2,1)} %param.25) | copy-start | bytes 1156
  12.1 31.8 %copy-start = (f32[3,256,384]{2,1,0:T(8,128)S(1)}, f32[3,256,384]{2,1,0:T(8,128)}, u32[]{:S(2)}) copy-start(f32[3,256,384]{2,1,0:T(8,128)} %param.13) | copy-start | bytes 3538948
  12.1 132.3 %all-gather.33.cloned.1.call-start = ((), (), s32[]{:S(2)}) async-start(), calls=%async_computation.24 | async-start | bytes 1474560 | tf_op jit(solution)/shard_map/all_gather | solution.py:266
  12.7 136.6 %all-gather.35.cloned.1.call-start = ((), (), s32[]{:S(2)}) async-start(), calls=%async_computation.25 | async-start | bytes 1474560 | tf_op jit(solution)/shard_map/all_gather | solution.py:268
  13.5 74.6 %copy-start.39 = (bf16[1,96,1152]{2,1,0:T(8,128)(2,1)}, bf16[1,96,1152]{2,1,0:T(8,128)(2,1)S(1)}, u32[]{:S(2)}) copy-start(bf16[1,96,1152]{2,1,0:T(8,128)(2,1)S(1)} %get-tuple-element.85) | copy-start | bytes 663556
  13.5 52.8 %collective-permute-start = (bf16[1,96,1152]{2,1,0:T(8,128)(2,1)S(1)}, bf16[1,96,1152]{2,1,0:T(8,128)(2,1)S(1)}, u32[]{:S(2)}, u32[]{:S(2)}) collective-permute-start(bf16[1,96,1152]{2,1,0:T(8,128)(2,1)S(1)} %get-tuple-element.86), channel_id=1, source_target_pairs={{0,1},{1,0},{2,3},{3,2},{4,5},{5,4},{6,7},{7,6},{8,9},{9,8},{10,11... | collective-permute-start | bytes 663560 | tf_op jit(solution)/shard_map/ppermute | solution.py:24
  14.1 340.5 %reduce-scatter.21.cloned.1.call-start = ((), (), s32[]{:S(2)}) async-start(), calls=%async_computation.15 | async-start | bytes 737280 | tf_op jit(solution)/shard_map/reduce_scatter | solution.py:303
  14.1 30.3 %copy-start.71 = (bf16[2,96,384]{2,1,0:T(8,128)(2,1)S(1)}, bf16[2,96,384]{2,1,0:T(8,128)(2,1)}, u32[]{:S(2)}) copy-start(bf16[2,96,384]{2,1,0:T(8,128)(2,1)} %param.20) | copy-start | bytes 442372
  26.4 25.8 %copy-start.120 = (bf16[2,384]{1,0:T(2,128)(2,1)S(1)}, bf16[2,384]{1,0:T(2,128)(2,1)}, u32[]{:S(2)}) copy-start(bf16[2,384]{1,0:T(2,128)(2,1)} %param.23) | copy-start | bytes 4612
  44.0 57.2 %copy-start.80 = (f32[3,256]{1,0:T(4,128)}, f32[3,256]{1,0:T(4,128)S(1)}, u32[]{:S(2)}) copy-start(f32[3,256]{1,0:T(4,128)S(1)} %broadcast_multiply_fusion.13) | copy-start | bytes 9220
  51.6 63.5 %copy-start.13 = (bf16[1,384,384]{2,1,0:T(8,128)(2,1)}, bf16[1,384,384]{2,1,0:T(8,128)(2,1)S(1)}, u32[]{:S(2)}) copy-start(bf16[1,384,384]{2,1,0:T(8,128)(2,1)S(1)} %all-gather.2) | copy-start | bytes 884740
  66.3 34.9 %copy-start.89 = (f32[3,256]{1,0:T(4,128)}, f32[3,256]{1,0:T(4,128)S(1)}, u32[]{:S(2)}) copy-start(f32[3,256]{1,0:T(4,128)S(1)} %add_rsqrt_fusion.5) | copy-start | bytes 9220
  66.5 31.6 %collective-permute-start.1 = (bf16[2,96,1152]{2,1,0:T(8,128)(2,1)S(1)}, bf16[2,96,1152]{2,1,0:T(8,128)(2,1)S(1)}, u32[]{:S(2)}, u32[]{:S(2)}) collective-permute-start(bf16[2,96,1152]{2,1,0:T(8,128)(2,1)S(1)} %get-tuple-element.88), channel_id=1, source_target_pairs={{0,2},{1,3},{2,0},{3,1},{4,6},{5,7},{6,4},{7,5},{8,10},{9,11},{10,... | collective-permute-start | bytes 1327112 | tf_op jit(solution)/shard_map/ppermute | solution.py:24
  101.5 6.2 copy-start.42
  119.2 23.1 %copy-start.66 = (f32[3,384]{1,0:T(4,128)}, f32[3,384]{1,0:T(4,128)S(1)}, u32[]{:S(2)}) copy-start(f32[3,384]{1,0:T(4,128)S(1)} %get-tuple-element.96) | copy-start | bytes 13828
  144.1 15.0 %copy-start.1 = (f32[3,256,384]{2,1,0:T(8,128)}, f32[3,256,384]{2,1,0:T(8,128)S(1)}, u32[]{:S(2)}) copy-start(f32[3,256,384]{2,1,0:T(8,128)S(1)} %get-tuple-element.73) | copy-start | bytes 3538948
  144.4 14.7 %copy-start.74 = (f32[3,256]{1,0:T(4,128)}, f32[3,256]{1,0:T(4,128)S(1)}, u32[]{:S(2)}) copy-start(f32[3,256]{1,0:T(4,128)S(1)} %add_rsqrt_fusion.1) | copy-start | bytes 9220
  149.3 7.6 copy-start.33
  149.3 7.6 copy-start.78
  180.7 9.0 %copy-start.35 = (bf16[1,384,1152]{2,1,0:T(8,128)(2,1)S(1)}, bf16[1,384,1152]{2,1,0:T(8,128)(2,1)}, u32[]{:S(2)}) copy-start(bf16[1,384,1152]{2,1,0:T(8,128)(2,1)} %all-gather.17) | copy-start | bytes 2654212
  208.8 5.2 copy-start.23
  215.9 138.6 %reduce-scatter.19.cloned.1.call-start = ((), (), s32[]{:S(2)}) async-start(), calls=%async_computation.14 | async-start | bytes 737280 | tf_op jit(solution)/shard_map/reduce_scatter | solution.py:303
  219.0 9.2 %copy-start.15 = (f32[3,256,384]{2,1,0:T(8,128)}, f32[3,256,384]{2,1,0:T(8,128)S(1)}, u32[]{:S(2)}) copy-start(f32[3,256,384]{2,1,0:T(8,128)S(1)} %get-tuple-element.67) | copy-start | bytes 3538948
  233.3 121.3 %reduce-scatter.17.cloned.1.call-start = ((), (), s32[]{:S(2)}) async-start(), calls=%async_computation.13 | async-start | bytes 2211840 | tf_op jit(solution)/shard_map/reduce_scatter | solution.py:302
  237.2 117.3 %reduce-scatter.15.cloned.1.call-start = ((), (), s32[]{:S(2)}) async-start(), calls=%async_computation.12 | async-start | bytes 2211840 | tf_op jit(solution)/shard_map/reduce_scatter | solution.py:302
  272.1 90.5 %reduce-scatter.25.cloned.1.call-start = ((), (), s32[]{:S(2)}) async-start(), calls=%async_computation.17 | async-start | bytes 2949120 | tf_op jit(solution)/shard_map/reduce_scatter | solution.py:305
  277.8 120.0 %reduce-scatter.23.cloned.1.call-start = ((), (), s32[]{:S(2)}) async-start(), calls=%async_computation.16 | async-start | bytes 2949120 | tf_op jit(solution)/shard_map/reduce_scatter | solution.py:305
  282.9 150.3 %reduce-scatter.29.cloned.1.call-start = ((), (), s32[]{:S(2)}) async-start(), calls=%async_computation.19 | async-start | bytes 2949120 | tf_op jit(solution)/shard_map/reduce_scatter | solution.py:307
  290.2 178.2 %reduce-scatter.27.cloned.1.call-start = ((), (), s32[]{:S(2)}) async-start(), calls=%async_computation.18 | async-start | bytes 2949120 | tf_op jit(solution)/shard_map/reduce_scatter | solution.py:307
  297.8 213.4 %reduce-scatter.13.cloned.1.call-start = ((), (), s32[]{:S(2)}) async-start(), calls=%async_computation.11 | async-start | bytes 4423680 | tf_op jit(solution)/shard_map/reduce_scatter | solution.py:300
  298.5 8.1 %copy-start.125 = (f32[384]{0:T(512)}, f32[384]{0:T(512)S(1)}, u32[]{:S(2)}) copy-start(f32[384]{0:T(512)S(1)} %convert_element_type.236) | copy-start | bytes 4612
  301.4 5.9 copy-start.65
  309.7 244.3 %reduce-scatter.11.cloned.1.call-start = ((), (), s32[]{:S(2)}) async-start(), calls=%async_computation.10 | async-start | bytes 4423680 | tf_op jit(solution)/shard_map/reduce_scatter | solution.py:300
  310.4 5.0 copy-start.119
  310.4 5.0 copy-start.118
  310.4 5.0 copy-start.115
  310.4 5.0 copy-start.124
  310.4 5.0 copy-start.130
  322.8 422.1 %all-reduce.20.cloned.1.call-start = ((), (), s32[]{:S(2)}) async-start(), calls=%async_computation.26 | async-start | bytes 10616832 | tf_op jit(solution)/shard_map/psum | solution.py:310
  323.7 1.5 collective-permute-start.2
  326.1 12.6 %collective-permute-start.3 = (bf16[2,96,1152]{2,1,0:T(8,128)(2,1)}, bf16[2,96,1152]{2,1,0:T(8,128)(2,1)S(1)}, u32[]{:S(2)}, u32[]{:S(2)}) collective-permute-start(bf16[2,96,1152]{2,1,0:T(8,128)(2,1)} %get-tuple-element.82), channel_id=1, source_target_pairs={{0,2},{1,3},{2,0},{3,1},{4,6},{5,7},{6,4},{7,5},{8,10},{9,11},{10,... | collective-permute-start | bytes 1327112 | tf_op jit(solution)/shard_map/ppermute | solution.py:24
  (104 other events, 189.8 us)
Sparse Core Ops, SparseCore 0:
  10.1 24.3 all-gather.24
  36.7 23.0 all-gather.30
  61.9 24.6 all-gather.28
  88.5 17.4 all-gather.26
  108.0 17.4 all-gather.32
  127.5 17.3 all-gather.34
  216.1 22.7 reduce-scatter.20
  241.4 22.0 reduce-scatter.18
  266.1 29.1 reduce-scatter.16
  297.7 29.1 reduce-scatter.14
  329.5 33.0 reduce-scatter.24
  365.0 32.7 reduce-scatter.22
  400.3 32.8 reduce-scatter.28
  435.5 32.8 reduce-scatter.26
  470.8 40.3 reduce-scatter.12
  513.6 40.3 reduce-scatter.10
  558.7 186.2 all-reduce.19
